TPU v7x, 512 devices: a whole 4x4x16 slice. The times are simulated.
512 devices in a mesh: row: 16 (over x, y), col: 32 (over z, core).
Axes of the slice: x: 4, y: 4, z: 16, core: 2. Of those that a mesh axis runs over, the one named last changes fastest.
Arguments:
- positions: float32 [3, 32768], P(None, ('row', 'col')), may hold values from -1 to 96, as said below
- noise: float32 [8, 3, 32768], P(None, None, ('row', 'col')), may hold values from -6 to 6
Outputs:
- basis: float32 [8, 3, 32768], P(None, None, ('row', 'col'))
- residual: float32 [8, 3, 32768], P(None, None, ('row', 'col'))
- coefficients: float32 [3, 8, 8], replicated
Inputs may be any that keep to these rules, and one draw needn't show every extreme that they name: `positions`: bead k lies within 0.77 of each coordinate of its own point of a cubic lattice of spacing 2.2 with 32 by 32 points a layer, distinct beads on distinct points.
All inputs are finite; a program needn't handle non-finite values.
Results may differ from a plain program's by a relative error of at most 0.0003.
Values sent between devices are 32-bit elements; how exact they have to be, the bound alone decides.
A program may use at most 64 MiB of HBM per device.

v0:
```python
import jax
import jax.numpy as jnp
from jax import lax
from jax.sharding import PartitionSpec as P


def pair_tensor(target_pos, source_pos):
    displace = target_pos[:, :, None] - source_pos[:, None, :]
    distance_sq = jnp.sum(displace * displace, axis=0)
    distance = jnp.sqrt(distance_sq)
    safe_distance = jnp.where(distance > 0, distance, 1.0)
    safe_sq = safe_distance * safe_distance
    far_iso = 0.75 / safe_distance * (1.0 + 2.0 / (3.0 * safe_sq))
    far_dir = 0.75 / safe_distance * (1.0 - 2.0 / safe_sq) / safe_sq
    near_iso = 1.0 - 9.0 * distance / 32.0
    near_dir = 3.0 / (32.0 * safe_distance)
    intersecting = distance < 2.0
    iso_part = jnp.where(intersecting, near_iso, far_iso)
    dir_part = jnp.where(intersecting, near_dir, far_dir)
    identity = jnp.eye(3, dtype=displace.dtype)
    return identity[:, :, None, None] * iso_part + dir_part * displace[:, None] * displace[None, :]


def local_gram(left, right):
    return jnp.einsum("kan,jan->kj", left, right, precision=lax.Precision.HIGHEST)


def combine(vectors, matrix):
    return jnp.einsum("kan,kj->jan", vectors, matrix, precision=lax.Precision.HIGHEST)


def lower_inverse(factor):
    return jax.scipy.linalg.solve_triangular(
        factor, jnp.eye(factor.shape[0], dtype=factor.dtype), lower=True
    )


def local(positions, noise):
    local_beads = positions.shape[1]
    total_count = 3.0 * local_beads * lax.axis_size("row") * lax.axis_size("col")
    target_pos = lax.all_gather(positions, "row", axis=1, tiled=True)
    source_pos = lax.all_gather(positions, "col", axis=1, tiled=True)

    def mobility(vectors):
        initial = jnp.zeros((vectors.shape[0], 3, target_pos.shape[1]), jnp.float32)
        source_piece = lax.all_gather(vectors, "col", axis=2, tiled=True)
        piece_width = source_piece.shape[2]
        block_count = 1
        while piece_width % block_count != 0 or piece_width // block_count > 256:
            block_count = block_count + 1
        block_width = piece_width // block_count

        def add_block(block_index, running):
            block_pos = lax.dynamic_slice_in_dim(
                source_pos, block_index * block_width, block_width, 1
            )
            block_vectors = lax.dynamic_slice_in_dim(
                source_piece, block_index * block_width, block_width, 2
            )
            tensor = pair_tensor(target_pos, block_pos)
            return running + jnp.einsum(
                "abts,kbs->kat", tensor, block_vectors, precision=lax.Precision.HIGHEST
            )

        partial_image = lax.fori_loop(0, block_count, add_block, initial)
        summed = lax.psum(partial_image, "row")
        return lax.dynamic_slice_in_dim(summed, lax.axis_index("row") * local_beads, local_beads, 2)

    start_matrix = lax.psum(local_gram(noise, noise), ("row", "col")) / total_count
    start_factor = jnp.linalg.cholesky(start_matrix)
    first = combine(noise, lower_inverse(start_factor).T)
    image = mobility(first)
    alpha_one = lax.psum(local_gram(first, image), ("row", "col")) / total_count
    remainder = image - combine(first, alpha_one)
    residual_matrix = lax.psum(local_gram(remainder, remainder), ("row", "col")) / total_count
    factor_one = jnp.linalg.cholesky(residual_matrix)
    basis = combine(remainder, lower_inverse(factor_one).T)
    image = mobility(basis) - combine(first, factor_one)
    alpha_two = lax.psum(local_gram(basis, image), ("row", "col")) / total_count
    residual = image - combine(basis, alpha_two)
    return (basis, residual, jnp.stack([alpha_one, factor_one, alpha_two]))


def solution(mesh):
    return jax.shard_map(
        local,
        mesh=mesh,
        in_specs=(P(None, ("row", "col")), P(None, None, ("row", "col"))),
        out_specs=(P(None, None, ("row", "col")), P(None, None, ("row", "col")), P()),
        check_vma=False,
    )
```

profile of v0, /device:TPU:1, one launch (start us, length us, event | category | flops | bytes accessed | tf_op | source)
XLA Modules:
  0.0 1041.4 jit_solution(14341036072423276544)
XLA Ops:
  7.2 38.0 %all-gather.1 = f32[32,64,3]{1,2,0:T(4,128)S(1)} all-gather(f32[1,64,3]{1,2,0:T(4,128)} %bitcast.96), channel_id=1, replica_groups=mesh['row'=16,'col'=32] {'col'}, dimensions={0}, use_global_device_ids=true | all-gather | bytes 25344 | tf_op jit(solution)/shard_map/all_gather | solution.py:42
  45.2 18.3 %all-gather = f32[16,64,3]{1,2,0:T(4,128)S(1)} all-gather(f32[1,64,3]{1,2,0:T(4,128)} %bitcast.97), channel_id=1, replica_groups=mesh['row'=16,'col'=32] {'row'}, dimensions={0}, use_global_device_ids=true | all-gather | bytes 13056 | tf_op jit(solution)/shard_map/all_gather | solution.py:41
  63.7 104.2 %psum.42 = f32[8,8]{0,1:T(8,128)S(1)} all-reduce(f32[8,8]{0,1:T(8,128)S(1)} %convolution_bitcast_fusion.5), channel_id=1, replica_groups=mesh['row'=16,'col'=32] {'row','col'}, use_global_device_ids=true, to_apply=%region_0.0 | all-reduce | flops 64 | bytes 512 | tf_op jit(solution)/shard_map/psum | solution.py:69
  171.1 44.3 %all_gather.12 = f32[8,3,2048]{0,1,2:T(4,128)} all-gather(f32[8,3,64]{0,1,2:T(4,128)S(1)} %copy.36), channel_id=1, replica_groups=mesh['row'=16,'col'=32] {'col'}, dimensions={2}, use_global_device_ids=true | all-gather | bytes 202752 | tf_op jit(solution)/shard_map/all_gather | solution.py:46
  215.4 3.3 copy.39
  218.9 120.9 %while.32 = (s32[]{:T(128)}, f32[8,3,1024]{2,0,1:T(8,128)S(1)}, f32[8,3,2048]{2,0,1:T(8,128)S(1)}, f32[3,1024]{1,0:T(4,128)S(1)}, f32[3,2048]{1,0:T(4,128)S(1)},...) while((s32[]{:T(128)}, f32[8,3,1024]{2,0,1:T(8,128)S(1)}, f32[8,3,2048]{2,0,1:T(8,128)S(1)}, ...), condition=%wide.region_5.8_spmd.clone, body=%wide.region_3.7_spmd.clone.sunk | while | flops 242270240 | bytes 19134656 | solution.py:65
  221.4 2.1 subtract_multiply_fusion.4
  223.5 10.5 %fusion.87 = f32[8,3,1024]{2,0,1:T(8,128)S(1)} fusion(f32[3,1024,256]{2,1,0:T(8,128)} %get-tuple-element.423, f32[3,1024,256]{2,1,0:T(8,128)S(1)} %get-tuple-element.424, f32[1024,256]{1,0:T(8,128)} %get-tuple-element.425, f32[3,3]{1,0:T(4,128)S(1)} %fusion.86, f32[8,3,1024]{2,0,1:T(8,128)S(1)} %get-tuple-element.445, pred[]{:T(512)S(6)} %compare.14, ...), kind=kOutput, calls=%fused_computation.13.clone.1 | convolution fusion | flops 233619456 | bytes 7563269 | tf_op jit(solution)/shard_map/while/body/eval_jaxpr/abts,kbs->kat/dot_general | solution.py:61
  236.5 2.1 subtract_multiply_fusion.4
  238.7 10.5 %fusion.87 = f32[8,3,1024]{2,0,1:T(8,128)S(1)} fusion(f32[3,1024,256]{2,1,0:T(8,128)} %get-tuple-element.423, f32[3,1024,256]{2,1,0:T(8,128)S(1)} %get-tuple-element.424, f32[1024,256]{1,0:T(8,128)} %get-tuple-element.425, f32[3,3]{1,0:T(4,128)S(1)} %fusion.86, f32[8,3,1024]{2,0,1:T(8,128)S(1)} %get-tuple-element.445, pred[]{:T(512)S(6)} %compare.14, ...), kind=kOutput, calls=%fused_computation.13.clone.1 | convolution fusion | flops 233619456 | bytes 7563269 | tf_op jit(solution)/shard_map/while/body/eval_jaxpr/abts,kbs->kat/dot_general | solution.py:61
  253.8 10.5 %fusion.87 = f32[8,3,1024]{2,0,1:T(8,128)S(1)} fusion(f32[3,1024,256]{2,1,0:T(8,128)} %get-tuple-element.423, f32[3,1024,256]{2,1,0:T(8,128)S(1)} %get-tuple-element.424, f32[1024,256]{1,0:T(8,128)} %get-tuple-element.425, f32[3,3]{1,0:T(4,128)S(1)} %fusion.86, f32[8,3,1024]{2,0,1:T(8,128)S(1)} %get-tuple-element.445, pred[]{:T(512)S(6)} %compare.14, ...), kind=kOutput, calls=%fused_computation.13.clone.1 | convolution fusion | flops 233619456 | bytes 7563269 | tf_op jit(solution)/shard_map/while/body/eval_jaxpr/abts,kbs->kat/dot_general | solution.py:61
  268.9 10.5 %fusion.87 = f32[8,3,1024]{2,0,1:T(8,128)S(1)} fusion(f32[3,1024,256]{2,1,0:T(8,128)} %get-tuple-element.423, f32[3,1024,256]{2,1,0:T(8,128)S(1)} %get-tuple-element.424, f32[1024,256]{1,0:T(8,128)} %get-tuple-element.425, f32[3,3]{1,0:T(4,128)S(1)} %fusion.86, f32[8,3,1024]{2,0,1:T(8,128)S(1)} %get-tuple-element.445, pred[]{:T(512)S(6)} %compare.14, ...), kind=kOutput, calls=%fused_computation.13.clone.1 | convolution fusion | flops 233619456 | bytes 7563269 | tf_op jit(solution)/shard_map/while/body/eval_jaxpr/abts,kbs->kat/dot_general | solution.py:61
  284.0 10.5 %fusion.87 = f32[8,3,1024]{2,0,1:T(8,128)S(1)} fusion(f32[3,1024,256]{2,1,0:T(8,128)} %get-tuple-element.423, f32[3,1024,256]{2,1,0:T(8,128)S(1)} %get-tuple-element.424, f32[1024,256]{1,0:T(8,128)} %get-tuple-element.425, f32[3,3]{1,0:T(4,128)S(1)} %fusion.86, f32[8,3,1024]{2,0,1:T(8,128)S(1)} %get-tuple-element.445, pred[]{:T(512)S(6)} %compare.14, ...), kind=kOutput, calls=%fused_computation.13.clone.1 | convolution fusion | flops 233619456 | bytes 7563269 | tf_op jit(solution)/shard_map/while/body/eval_jaxpr/abts,kbs->kat/dot_general | solution.py:61
  299.1 10.5 %fusion.87 = f32[8,3,1024]{2,0,1:T(8,128)S(1)} fusion(f32[3,1024,256]{2,1,0:T(8,128)} %get-tuple-element.423, f32[3,1024,256]{2,1,0:T(8,128)S(1)} %get-tuple-element.424, f32[1024,256]{1,0:T(8,128)} %get-tuple-element.425, f32[3,3]{1,0:T(4,128)S(1)} %fusion.86, f32[8,3,1024]{2,0,1:T(8,128)S(1)} %get-tuple-element.445, pred[]{:T(512)S(6)} %compare.14, ...), kind=kOutput, calls=%fused_computation.13.clone.1 | convolution fusion | flops 233619456 | bytes 7563269 | tf_op jit(solution)/shard_map/while/body/eval_jaxpr/abts,kbs->kat/dot_general | solution.py:61
  314.2 10.5 %fusion.87 = f32[8,3,1024]{2,0,1:T(8,128)S(1)} fusion(f32[3,1024,256]{2,1,0:T(8,128)} %get-tuple-element.423, f32[3,1024,256]{2,1,0:T(8,128)S(1)} %get-tuple-element.424, f32[1024,256]{1,0:T(8,128)} %get-tuple-element.425, f32[3,3]{1,0:T(4,128)S(1)} %fusion.86, f32[8,3,1024]{2,0,1:T(8,128)S(1)} %get-tuple-element.445, pred[]{:T(512)S(6)} %compare.14, ...), kind=kOutput, calls=%fused_computation.13.clone.1 | convolution fusion | flops 233619456 | bytes 7563269 | tf_op jit(solution)/shard_map/while/body/eval_jaxpr/abts,kbs->kat/dot_general | solution.py:61
  329.4 10.5 %fusion.87 = f32[8,3,1024]{2,0,1:T(8,128)S(1)} fusion(f32[3,1024,256]{2,1,0:T(8,128)} %get-tuple-element.423, f32[3,1024,256]{2,1,0:T(8,128)S(1)} %get-tuple-element.424, f32[1024,256]{1,0:T(8,128)} %get-tuple-element.425, f32[3,3]{1,0:T(4,128)S(1)} %fusion.86, f32[8,3,1024]{2,0,1:T(8,128)S(1)} %get-tuple-element.445, pred[]{:T(512)S(6)} %compare.14, ...), kind=kOutput, calls=%fused_computation.13.clone.1 | convolution fusion | flops 233619456 | bytes 7563269 | tf_op jit(solution)/shard_map/while/body/eval_jaxpr/abts,kbs->kat/dot_general | solution.py:61
  340.6 103.5 %all-reduce.3.cloned.1.call-done = f32[8,3,1024]{2,0,1:T(8,128)} async-done(((f32[8,3,1024]{2,0,1:T(8,128)}), f32[8,3,1024]{2,0,1:T(8,128)}) %all-reduce.3.cloned.1.call-update) | async-done | bytes 98320 | tf_op jit(solution)/shard_map/psum | solution.py:66
  444.9 104.2 %psum.44 = f32[8,8]{0,1:T(8,128)S(1)} all-reduce(f32[8,8]{0,1:T(8,128)S(1)} %convolution_bitcast_fusion.3), channel_id=1, replica_groups=mesh['row'=16,'col'=32] {'row','col'}, use_global_device_ids=true, to_apply=%region_7.10 | all-reduce | flops 64 | bytes 512 | tf_op jit(solution)/shard_map/psum | solution.py:73
  550.1 100.2 %psum.45 = f32[8,8]{0,1:T(8,128)S(1)} all-reduce(f32[8,8]{0,1:T(8,128)S(1)} %convolution_bitcast_fusion.2), channel_id=1, replica_groups=mesh['row'=16,'col'=32] {'row','col'}, use_global_device_ids=true, to_apply=%region_8.11 | all-reduce | flops 64 | bytes 512 | tf_op jit(solution)/shard_map/psum | solution.py:75
  653.5 43.3 %all_gather.15 = f32[8,3,2048]{0,1,2:T(4,128)} all-gather(f32[8,3,64]{0,1,2:T(4,128)S(1)} %copy.44), channel_id=1, replica_groups=mesh['row'=16,'col'=32] {'col'}, dimensions={2}, use_global_device_ids=true | all-gather | bytes 202752 | tf_op jit(solution)/shard_map/all_gather | solution.py:46
  696.8 3.3 copy.45
  700.1 120.9 %while.33 = (s32[]{:T(128)}, f32[8,3,1024]{2,0,1:T(8,128)S(1)}, f32[8,3,2048]{2,0,1:T(8,128)S(1)}, f32[3,1024]{1,0:T(4,128)S(1)}, f32[3,2048]{1,0:T(4,128)S(1)},...) while((s32[]{:T(128)}, f32[8,3,1024]{2,0,1:T(8,128)S(1)}, f32[8,3,2048]{2,0,1:T(8,128)S(1)}, ...), condition=%wide.region_11.14_spmd.clone, body=%wide.region_9.13_spmd.clone.sunk | while | flops 242270240 | bytes 19134656 | solution.py:65
  704.8 10.5 %fusion.91 = f32[8,3,1024]{2,0,1:T(8,128)S(1)} fusion(f32[3,1024,256]{2,1,0:T(8,128)} %get-tuple-element.432, f32[3,1024,256]{2,1,0:T(8,128)S(1)} %get-tuple-element.433, f32[1024,256]{1,0:T(8,128)} %get-tuple-element.434, f32[3,3]{1,0:T(4,128)S(1)} %fusion.90, f32[8,3,1024]{2,0,1:T(8,128)S(1)} %get-tuple-element.472, pred[]{:T(512)S(6)} %compare.15, ...), kind=kOutput, calls=%fused_computation.37.clone.1 | convolution fusion | flops 233619456 | bytes 7563269 | tf_op jit(solution)/shard_map/while/body/eval_jaxpr/abts,kbs->kat/dot_general | solution.py:61
  719.9 10.5 %fusion.91 = f32[8,3,1024]{2,0,1:T(8,128)S(1)} fusion(f32[3,1024,256]{2,1,0:T(8,128)} %get-tuple-element.432, f32[3,1024,256]{2,1,0:T(8,128)S(1)} %get-tuple-element.433, f32[1024,256]{1,0:T(8,128)} %get-tuple-element.434, f32[3,3]{1,0:T(4,128)S(1)} %fusion.90, f32[8,3,1024]{2,0,1:T(8,128)S(1)} %get-tuple-element.472, pred[]{:T(512)S(6)} %compare.15, ...), kind=kOutput, calls=%fused_computation.37.clone.1 | convolution fusion | flops 233619456 | bytes 7563269 | tf_op jit(solution)/shard_map/while/body/eval_jaxpr/abts,kbs->kat/dot_general | solution.py:61
  735.0 10.5 %fusion.91 = f32[8,3,1024]{2,0,1:T(8,128)S(1)} fusion(f32[3,1024,256]{2,1,0:T(8,128)} %get-tuple-element.432, f32[3,1024,256]{2,1,0:T(8,128)S(1)} %get-tuple-element.433, f32[1024,256]{1,0:T(8,128)} %get-tuple-element.434, f32[3,3]{1,0:T(4,128)S(1)} %fusion.90, f32[8,3,1024]{2,0,1:T(8,128)S(1)} %get-tuple-element.472, pred[]{:T(512)S(6)} %compare.15, ...), kind=kOutput, calls=%fused_computation.37.clone.1 | convolution fusion | flops 233619456 | bytes 7563269 | tf_op jit(solution)/shard_map/while/body/eval_jaxpr/abts,kbs->kat/dot_general | solution.py:61
  750.1 10.5 %fusion.91 = f32[8,3,1024]{2,0,1:T(8,128)S(1)} fusion(f32[3,1024,256]{2,1,0:T(8,128)} %get-tuple-element.432, f32[3,1024,256]{2,1,0:T(8,128)S(1)} %get-tuple-element.433, f32[1024,256]{1,0:T(8,128)} %get-tuple-element.434, f32[3,3]{1,0:T(4,128)S(1)} %fusion.90, f32[8,3,1024]{2,0,1:T(8,128)S(1)} %get-tuple-element.472, pred[]{:T(512)S(6)} %compare.15, ...), kind=kOutput, calls=%fused_computation.37.clone.1 | convolution fusion | flops 233619456 | bytes 7563269 | tf_op jit(solution)/shard_map/while/body/eval_jaxpr/abts,kbs->kat/dot_general | solution.py:61
  765.2 10.5 %fusion.91 = f32[8,3,1024]{2,0,1:T(8,128)S(1)} fusion(f32[3,1024,256]{2,1,0:T(8,128)} %get-tuple-element.432, f32[3,1024,256]{2,1,0:T(8,128)S(1)} %get-tuple-element.433, f32[1024,256]{1,0:T(8,128)} %get-tuple-element.434, f32[3,3]{1,0:T(4,128)S(1)} %fusion.90, f32[8,3,1024]{2,0,1:T(8,128)S(1)} %get-tuple-element.472, pred[]{:T(512)S(6)} %compare.15, ...), kind=kOutput, calls=%fused_computation.37.clone.1 | convolution fusion | flops 233619456 | bytes 7563269 | tf_op jit(solution)/shard_map/while/body/eval_jaxpr/abts,kbs->kat/dot_general | solution.py:61
  780.4 10.5 %fusion.91 = f32[8,3,1024]{2,0,1:T(8,128)S(1)} fusion(f32[3,1024,256]{2,1,0:T(8,128)} %get-tuple-element.432, f32[3,1024,256]{2,1,0:T(8,128)S(1)} %get-tuple-element.433, f32[1024,256]{1,0:T(8,128)} %get-tuple-element.434, f32[3,3]{1,0:T(4,128)S(1)} %fusion.90, f32[8,3,1024]{2,0,1:T(8,128)S(1)} %get-tuple-element.472, pred[]{:T(512)S(6)} %compare.15, ...), kind=kOutput, calls=%fused_computation.37.clone.1 | convolution fusion | flops 233619456 | bytes 7563269 | tf_op jit(solution)/shard_map/while/body/eval_jaxpr/abts,kbs->kat/dot_general | solution.py:61
  795.5 10.5 %fusion.91 = f32[8,3,1024]{2,0,1:T(8,128)S(1)} fusion(f32[3,1024,256]{2,1,0:T(8,128)} %get-tuple-element.432, f32[3,1024,256]{2,1,0:T(8,128)S(1)} %get-tuple-element.433, f32[1024,256]{1,0:T(8,128)} %get-tuple-element.434, f32[3,3]{1,0:T(4,128)S(1)} %fusion.90, f32[8,3,1024]{2,0,1:T(8,128)S(1)} %get-tuple-element.472, pred[]{:T(512)S(6)} %compare.15, ...), kind=kOutput, calls=%fused_computation.37.clone.1 | convolution fusion | flops 233619456 | bytes 7563269 | tf_op jit(solution)/shard_map/while/body/eval_jaxpr/abts,kbs->kat/dot_general | solution.py:61
  810.6 10.5 %fusion.91 = f32[8,3,1024]{2,0,1:T(8,128)S(1)} fusion(f32[3,1024,256]{2,1,0:T(8,128)} %get-tuple-element.432, f32[3,1024,256]{2,1,0:T(8,128)S(1)} %get-tuple-element.433, f32[1024,256]{1,0:T(8,128)} %get-tuple-element.434, f32[3,3]{1,0:T(4,128)S(1)} %fusion.90, f32[8,3,1024]{2,0,1:T(8,128)S(1)} %get-tuple-element.472, pred[]{:T(512)S(6)} %compare.15, ...), kind=kOutput, calls=%fused_computation.37.clone.1 | convolution fusion | flops 233619456 | bytes 7563269 | tf_op jit(solution)/shard_map/while/body/eval_jaxpr/abts,kbs->kat/dot_general | solution.py:61
  821.8 105.6 %all-reduce.5.cloned.1.call-done = f32[8,3,1024]{2,0,1:T(8,128)} async-done(((f32[8,3,1024]{2,0,1:T(8,128)}), f32[8,3,1024]{2,0,1:T(8,128)}) %all-reduce.5.cloned.1.call-update) | async-done | bytes 98320 | tf_op jit(solution)/shard_map/psum | solution.py:66
  929.1 104.0 %psum.47 = f32[8,8]{0,1:T(8,128)S(1)} all-reduce(f32[8,8]{0,1:T(8,128)S(1)} %convolution_bitcast_fusion), channel_id=1, replica_groups=mesh['row'=16,'col'=32] {'row','col'}, use_global_device_ids=true, to_apply=%region_13.16 | all-reduce | flops 64 | bytes 512 | tf_op jit(solution)/shard_map/psum | solution.py:79
  (130 shorter events, 83.1 us)
Async XLA Ops:
  7.2 56.4 %copy-start = (f32[8,3,64]{2,0,1:T(8,128)S(1)}, f32[8,3,64]{2,0,1:T(8,128)}, u32[]{:S(2)}) copy-start(f32[8,3,64]{2,0,1:T(8,128)} %param.10) | copy-start | bytes 18436
  7.2 436.9 %all-reduce.3.cloned.1.call-start = ((), (), s32[]{:S(2)}) async-start(), calls=%async_computation | async-start | bytes 196608 | tf_op jit(solution)/shard_map/psum | solution.py:66
  339.8 0.6 copy-start.3
  340.5 586.9 %all-reduce.5.cloned.1.call-start = ((), (), s32[]{:S(2)}) async-start(), calls=%async_computation.1 | async-start | bytes 196608 | tf_op jit(solution)/shard_map/psum | solution.py:66
  653.4 379.7 %copy-start.1 = (f32[8,3,64]{2,0,1:T(8,128)}, f32[8,3,64]{2,0,1:T(8,128)S(1)}, u32[]{:S(2)}) copy-start(f32[8,3,64]{2,0,1:T(8,128)S(1)} %fusion.61) | copy-start | bytes 18436
  821.0 0.6 copy-start.2
Sparse Core Ops, SparseCore 0:
  340.6 103.3 all-reduce.2
  821.8 105.5 all-reduce.4
where the time goes:
time: 1040 us
  blocking collectives  556 us (53%)
  waiting for transfers between devices  209 us (20%)
  matrix products  173 us (17%)
  other arithmetic  80.1 us (8%)
  between operations  14.1 us (1%)
    psum x2, waiting for transfers between devices, mobility(): summed = lax.psum(partial_image, 'row')  209 us
    dot_general x16, matrix products, add_block(): jnp.einsum('abts,kbs->kat', tensor, block_vectors, precision=lax.Precisio...  168 us
    psum x1, blocking collectives, local(): lax.psum(local_gram(noise, noise), ('row', 'col')) / total_count  104 us
    psum x1, blocking collectives, local(): alpha_one = lax.psum(local_gram(first, image), ('row', 'col')) / total_count  104 us
    psum x1, blocking collectives, local(): alpha_two = lax.psum(local_gram(basis, image), ('row', 'col')) / total_count  104 us
    psum x1, blocking collectives, local(): lax.psum(local_gram(remainder, remainder), ('row', 'col')) / total_count  100 us
    all_gather x2, blocking collectives, mobility(): source_piece = lax.all_gather(vectors, 'col', axis=2, tiled=True)  87.6 us
    all_gather x1, blocking collectives, local(): source_pos = lax.all_gather(positions, 'col', axis=1, tiled=True)  38 us
  transfers between devices with their start and end apart: 2, of which 2 were waited for; matrix products, arithmetic and copies ran while one was open for 0% of the time, Pallas kernels for 0%

commit v1 on v0

--- a/solution.py
+++ b/solution.py
@@ -66,7 +66,7 @@
         summed = lax.psum(partial_image, "row")
         return lax.dynamic_slice_in_dim(summed, lax.axis_index("row") * local_beads, local_beads, 2)
 
-    start_matrix = lax.psum(local_gram(noise, noise), ("row", "col")) / total_count
+    start_matrix = lax.psum(lax.psum(local_gram(noise, noise), "row"), "col") / total_count
     start_factor = jnp.linalg.cholesky(start_matrix)
     first = combine(noise, lower_inverse(start_factor).T)
     image = mobility(first)

time: 1040 us -> 1030 us (level)
  blocking collectives: 556 us -> 541 us
    psum x1 -> x2, blocking collectives: 104 us -> 88.8 us  [the longest x1 57.9 us: local(): lax.psum(lax.psum(local_gram(noise, noise), 'row'), 'col') / total_count]
where the time goes in v1:
time: 1030 us; the launch traced here: 1020 us
  blocking collectives  541 us (53%)
  waiting for transfers between devices  208 us (20%)
  matrix products  173 us (17%)
  other arithmetic  80.1 us (8%)
  between operations  14.1 us (1%)
    psum x2, waiting for transfers between devices, mobility(): summed = lax.psum(partial_image, 'row')  208 us
    dot_general x16, matrix products, add_block(): jnp.einsum('abts,kbs->kat', tensor, block_vectors, precision=lax.Precisio...  168 us
    psum x1, blocking collectives, local(): alpha_one = lax.psum(local_gram(first, image), ('row', 'col')) / total_count  104 us
    psum x1, blocking collectives, local(): alpha_two = lax.psum(local_gram(basis, image), ('row', 'col')) / total_count  104 us
    psum x1, blocking collectives, local(): lax.psum(local_gram(remainder, remainder), ('row', 'col')) / total_count  100 us
    all_gather x2, blocking collectives, mobility(): source_piece = lax.all_gather(vectors, 'col', axis=2, tiled=True)  87.1 us
    psum x1, blocking collectives, local(): lax.psum(lax.psum(local_gram(noise, noise), 'row'), 'col') / total_count  57.9 us
    all_gather x1, blocking collectives, local(): source_pos = lax.all_gather(positions, 'col', axis=1, tiled=True)  38 us
  transfers between devices with their start and end apart: 2, of which 2 were waited for; matrix products, arithmetic and copies ran while one was open for 0% of the time, Pallas kernels for 0%

profile of v1, /device:TPU:1, one launch (start us, length us, event | category | flops | bytes accessed | tf_op | source)
XLA Modules:
  0.0 1024.4 jit_solution(16390685396233314855)
XLA Ops:
  7.2 38.0 %all-gather.1 = f32[32,64,3]{1,2,0:T(4,128)S(1)} all-gather(f32[1,64,3]{1,2,0:T(4,128)} %bitcast.96), channel_id=1, replica_groups=mesh['row'=16,'col'=32] {'col'}, dimensions={0}, use_global_device_ids=true | all-gather | bytes 25344 | tf_op jit(solution)/shard_map/all_gather | solution.py:42
  45.2 18.3 %all-gather = f32[16,64,3]{1,2,0:T(4,128)S(1)} all-gather(f32[1,64,3]{1,2,0:T(4,128)} %bitcast.97), channel_id=1, replica_groups=mesh['row'=16,'col'=32] {'row'}, dimensions={0}, use_global_device_ids=true | all-gather | bytes 13056 | tf_op jit(solution)/shard_map/all_gather | solution.py:41
  63.7 30.9 %psum.49 = f32[8,8]{0,1:T(8,128)S(1)} all-reduce(f32[8,8]{0,1:T(8,128)S(1)} %convolution_bitcast_fusion.5), channel_id=1, replica_groups=mesh['row'=16,'col'=32] {'row'}, use_global_device_ids=true, to_apply=%region_0.0 | all-reduce | flops 64 | bytes 512 | tf_op jit(solution)/shard_map/psum | solution.py:69
  94.6 57.9 %psum.50 = f32[8,8]{0,1:T(8,128)S(1)} all-reduce(f32[8,8]{0,1:T(8,128)S(1)} %psum.49), channel_id=1, replica_groups=mesh['row'=16,'col'=32] {'col'}, use_global_device_ids=true, to_apply=%region_1.0 | all-reduce | flops 64 | bytes 512 | tf_op jit(solution)/shard_map/psum | solution.py:69
  155.7 43.8 %all_gather.12 = f32[8,3,2048]{0,1,2:T(4,128)} all-gather(f32[8,3,64]{0,1,2:T(4,128)S(1)} %copy.36), channel_id=1, replica_groups=mesh['row'=16,'col'=32] {'col'}, dimensions={2}, use_global_device_ids=true | all-gather | bytes 202752 | tf_op jit(solution)/shard_map/all_gather | solution.py:46
  199.5 3.3 copy.39
  203.0 120.9 %while.32 = (s32[]{:T(128)}, f32[8,3,1024]{2,0,1:T(8,128)S(1)}, f32[8,3,2048]{2,0,1:T(8,128)S(1)}, f32[3,1024]{1,0:T(4,128)S(1)}, f32[3,2048]{1,0:T(4,128)S(1)},...) while((s32[]{:T(128)}, f32[8,3,1024]{2,0,1:T(8,128)S(1)}, f32[8,3,2048]{2,0,1:T(8,128)S(1)}, ...), condition=%wide.region_6.9_spmd.clone, body=%wide.region_4.8_spmd.clone.sunk | while | flops 242270240 | bytes 19134656 | solution.py:65
  207.7 10.5 %fusion.87 = f32[8,3,1024]{2,0,1:T(8,128)S(1)} fusion(f32[3,1024,256]{2,1,0:T(8,128)} %get-tuple-element.423, f32[3,1024,256]{2,1,0:T(8,128)S(1)} %get-tuple-element.424, f32[1024,256]{1,0:T(8,128)} %get-tuple-element.425, f32[3,3]{1,0:T(4,128)S(1)} %fusion.86, f32[8,3,1024]{2,0,1:T(8,128)S(1)} %get-tuple-element.445, pred[]{:T(512)S(6)} %compare.14, ...), kind=kOutput, calls=%fused_computation.13.clone.1 | convolution fusion | flops 233619456 | bytes 7563269 | tf_op jit(solution)/shard_map/while/body/eval_jaxpr/abts,kbs->kat/dot_general | solution.py:61
  220.6 2.1 subtract_multiply_fusion.4
  222.8 10.5 %fusion.87 = f32[8,3,1024]{2,0,1:T(8,128)S(1)} fusion(f32[3,1024,256]{2,1,0:T(8,128)} %get-tuple-element.423, f32[3,1024,256]{2,1,0:T(8,128)S(1)} %get-tuple-element.424, f32[1024,256]{1,0:T(8,128)} %get-tuple-element.425, f32[3,3]{1,0:T(4,128)S(1)} %fusion.86, f32[8,3,1024]{2,0,1:T(8,128)S(1)} %get-tuple-element.445, pred[]{:T(512)S(6)} %compare.14, ...), kind=kOutput, calls=%fused_computation.13.clone.1 | convolution fusion | flops 233619456 | bytes 7563269 | tf_op jit(solution)/shard_map/while/body/eval_jaxpr/abts,kbs->kat/dot_general | solution.py:61
  237.9 10.5 %fusion.87 = f32[8,3,1024]{2,0,1:T(8,128)S(1)} fusion(f32[3,1024,256]{2,1,0:T(8,128)} %get-tuple-element.423, f32[3,1024,256]{2,1,0:T(8,128)S(1)} %get-tuple-element.424, f32[1024,256]{1,0:T(8,128)} %get-tuple-element.425, f32[3,3]{1,0:T(4,128)S(1)} %fusion.86, f32[8,3,1024]{2,0,1:T(8,128)S(1)} %get-tuple-element.445, pred[]{:T(512)S(6)} %compare.14, ...), kind=kOutput, calls=%fused_computation.13.clone.1 | convolution fusion | flops 233619456 | bytes 7563269 | tf_op jit(solution)/shard_map/while/body/eval_jaxpr/abts,kbs->kat/dot_general | solution.py:61
  253.0 10.5 %fusion.87 = f32[8,3,1024]{2,0,1:T(8,128)S(1)} fusion(f32[3,1024,256]{2,1,0:T(8,128)} %get-tuple-element.423, f32[3,1024,256]{2,1,0:T(8,128)S(1)} %get-tuple-element.424, f32[1024,256]{1,0:T(8,128)} %get-tuple-element.425, f32[3,3]{1,0:T(4,128)S(1)} %fusion.86, f32[8,3,1024]{2,0,1:T(8,128)S(1)} %get-tuple-element.445, pred[]{:T(512)S(6)} %compare.14, ...), kind=kOutput, calls=%fused_computation.13.clone.1 | convolution fusion | flops 233619456 | bytes 7563269 | tf_op jit(solution)/shard_map/while/body/eval_jaxpr/abts,kbs->kat/dot_general | solution.py:61
  268.1 10.5 %fusion.87 = f32[8,3,1024]{2,0,1:T(8,128)S(1)} fusion(f32[3,1024,256]{2,1,0:T(8,128)} %get-tuple-element.423, f32[3,1024,256]{2,1,0:T(8,128)S(1)} %get-tuple-element.424, f32[1024,256]{1,0:T(8,128)} %get-tuple-element.425, f32[3,3]{1,0:T(4,128)S(1)} %fusion.86, f32[8,3,1024]{2,0,1:T(8,128)S(1)} %get-tuple-element.445, pred[]{:T(512)S(6)} %compare.14, ...), kind=kOutput, calls=%fused_computation.13.clone.1 | convolution fusion | flops 233619456 | bytes 7563269 | tf_op jit(solution)/shard_map/while/body/eval_jaxpr/abts,kbs->kat/dot_general | solution.py:61
  283.2 10.5 %fusion.87 = f32[8,3,1024]{2,0,1:T(8,128)S(1)} fusion(f32[3,1024,256]{2,1,0:T(8,128)} %get-tuple-element.423, f32[3,1024,256]{2,1,0:T(8,128)S(1)} %get-tuple-element.424, f32[1024,256]{1,0:T(8,128)} %get-tuple-element.425, f32[3,3]{1,0:T(4,128)S(1)} %fusion.86, f32[8,3,1024]{2,0,1:T(8,128)S(1)} %get-tuple-element.445, pred[]{:T(512)S(6)} %compare.14, ...), kind=kOutput, calls=%fused_computation.13.clone.1 | convolution fusion | flops 233619456 | bytes 7563269 | tf_op jit(solution)/shard_map/while/body/eval_jaxpr/abts,kbs->kat/dot_general | solution.py:61
  298.4 10.5 %fusion.87 = f32[8,3,1024]{2,0,1:T(8,128)S(1)} fusion(f32[3,1024,256]{2,1,0:T(8,128)} %get-tuple-element.423, f32[3,1024,256]{2,1,0:T(8,128)S(1)} %get-tuple-element.424, f32[1024,256]{1,0:T(8,128)} %get-tuple-element.425, f32[3,3]{1,0:T(4,128)S(1)} %fusion.86, f32[8,3,1024]{2,0,1:T(8,128)S(1)} %get-tuple-element.445, pred[]{:T(512)S(6)} %compare.14, ...), kind=kOutput, calls=%fused_computation.13.clone.1 | convolution fusion | flops 233619456 | bytes 7563269 | tf_op jit(solution)/shard_map/while/body/eval_jaxpr/abts,kbs->kat/dot_general | solution.py:61
  313.5 10.5 %fusion.87 = f32[8,3,1024]{2,0,1:T(8,128)S(1)} fusion(f32[3,1024,256]{2,1,0:T(8,128)} %get-tuple-element.423, f32[3,1024,256]{2,1,0:T(8,128)S(1)} %get-tuple-element.424, f32[1024,256]{1,0:T(8,128)} %get-tuple-element.425, f32[3,3]{1,0:T(4,128)S(1)} %fusion.86, f32[8,3,1024]{2,0,1:T(8,128)S(1)} %get-tuple-element.445, pred[]{:T(512)S(6)} %compare.14, ...), kind=kOutput, calls=%fused_computation.13.clone.1 | convolution fusion | flops 233619456 | bytes 7563269 | tf_op jit(solution)/shard_map/while/body/eval_jaxpr/abts,kbs->kat/dot_general | solution.py:61
  324.7 102.4 %all-reduce.3.cloned.1.call-done = f32[8,3,1024]{2,0,1:T(8,128)} async-done(((f32[8,3,1024]{2,0,1:T(8,128)}), f32[8,3,1024]{2,0,1:T(8,128)}) %all-reduce.3.cloned.1.call-update) | async-done | bytes 98320 | tf_op jit(solution)/shard_map/psum | solution.py:66
  428.0 104.0 %psum.52 = f32[8,8]{0,1:T(8,128)S(1)} all-reduce(f32[8,8]{0,1:T(8,128)S(1)} %convolution_bitcast_fusion.3), channel_id=1, replica_groups=mesh['row'=16,'col'=32] {'row','col'}, use_global_device_ids=true, to_apply=%region_8.11 | all-reduce | flops 64 | bytes 512 | tf_op jit(solution)/shard_map/psum | solution.py:73
  532.9 100.4 %psum.53 = f32[8,8]{0,1:T(8,128)S(1)} all-reduce(f32[8,8]{0,1:T(8,128)S(1)} %convolution_bitcast_fusion.2), channel_id=1, replica_groups=mesh['row'=16,'col'=32] {'row','col'}, use_global_device_ids=true, to_apply=%region_9.12 | all-reduce | flops 64 | bytes 512 | tf_op jit(solution)/shard_map/psum | solution.py:75
  636.6 43.3 %all_gather.15 = f32[8,3,2048]{0,1,2:T(4,128)} all-gather(f32[8,3,64]{0,1,2:T(4,128)S(1)} %copy.44), channel_id=1, replica_groups=mesh['row'=16,'col'=32] {'col'}, dimensions={2}, use_global_device_ids=true | all-gather | bytes 202752 | tf_op jit(solution)/shard_map/all_gather | solution.py:46
  679.9 3.3 copy.45
  683.2 120.9 %while.33 = (s32[]{:T(128)}, f32[8,3,1024]{2,0,1:T(8,128)S(1)}, f32[8,3,2048]{2,0,1:T(8,128)S(1)}, f32[3,1024]{1,0:T(4,128)S(1)}, f32[3,2048]{1,0:T(4,128)S(1)},...) while((s32[]{:T(128)}, f32[8,3,1024]{2,0,1:T(8,128)S(1)}, f32[8,3,2048]{2,0,1:T(8,128)S(1)}, ...), condition=%wide.region_12.15_spmd.clone, body=%wide.region_10.14_spmd.clone.sunk | while | flops 242270240 | bytes 19134656 | solution.py:65
  687.8 10.5 %fusion.91 = f32[8,3,1024]{2,0,1:T(8,128)S(1)} fusion(f32[3,1024,256]{2,1,0:T(8,128)} %get-tuple-element.432, f32[3,1024,256]{2,1,0:T(8,128)S(1)} %get-tuple-element.433, f32[1024,256]{1,0:T(8,128)} %get-tuple-element.434, f32[3,3]{1,0:T(4,128)S(1)} %fusion.90, f32[8,3,1024]{2,0,1:T(8,128)S(1)} %get-tuple-element.472, pred[]{:T(512)S(6)} %compare.15, ...), kind=kOutput, calls=%fused_computation.37.clone.1 | convolution fusion | flops 233619456 | bytes 7563269 | tf_op jit(solution)/shard_map/while/body/eval_jaxpr/abts,kbs->kat/dot_general | solution.py:61
  702.9 10.5 %fusion.91 = f32[8,3,1024]{2,0,1:T(8,128)S(1)} fusion(f32[3,1024,256]{2,1,0:T(8,128)} %get-tuple-element.432, f32[3,1024,256]{2,1,0:T(8,128)S(1)} %get-tuple-element.433, f32[1024,256]{1,0:T(8,128)} %get-tuple-element.434, f32[3,3]{1,0:T(4,128)S(1)} %fusion.90, f32[8,3,1024]{2,0,1:T(8,128)S(1)} %get-tuple-element.472, pred[]{:T(512)S(6)} %compare.15, ...), kind=kOutput, calls=%fused_computation.37.clone.1 | convolution fusion | flops 233619456 | bytes 7563269 | tf_op jit(solution)/shard_map/while/body/eval_jaxpr/abts,kbs->kat/dot_general | solution.py:61
  718.1 10.5 %fusion.91 = f32[8,3,1024]{2,0,1:T(8,128)S(1)} fusion(f32[3,1024,256]{2,1,0:T(8,128)} %get-tuple-element.432, f32[3,1024,256]{2,1,0:T(8,128)S(1)} %get-tuple-element.433, f32[1024,256]{1,0:T(8,128)} %get-tuple-element.434, f32[3,3]{1,0:T(4,128)S(1)} %fusion.90, f32[8,3,1024]{2,0,1:T(8,128)S(1)} %get-tuple-element.472, pred[]{:T(512)S(6)} %compare.15, ...), kind=kOutput, calls=%fused_computation.37.clone.1 | convolution fusion | flops 233619456 | bytes 7563269 | tf_op jit(solution)/shard_map/while/body/eval_jaxpr/abts,kbs->kat/dot_general | solution.py:61
  733.2 10.5 %fusion.91 = f32[8,3,1024]{2,0,1:T(8,128)S(1)} fusion(f32[3,1024,256]{2,1,0:T(8,128)} %get-tuple-element.432, f32[3,1024,256]{2,1,0:T(8,128)S(1)} %get-tuple-element.433, f32[1024,256]{1,0:T(8,128)} %get-tuple-element.434, f32[3,3]{1,0:T(4,128)S(1)} %fusion.90, f32[8,3,1024]{2,0,1:T(8,128)S(1)} %get-tuple-element.472, pred[]{:T(512)S(6)} %compare.15, ...), kind=kOutput, calls=%fused_computation.37.clone.1 | convolution fusion | flops 233619456 | bytes 7563269 | tf_op jit(solution)/shard_map/while/body/eval_jaxpr/abts,kbs->kat/dot_general | solution.py:61
  748.3 10.5 %fusion.91 = f32[8,3,1024]{2,0,1:T(8,128)S(1)} fusion(f32[3,1024,256]{2,1,0:T(8,128)} %get-tuple-element.432, f32[3,1024,256]{2,1,0:T(8,128)S(1)} %get-tuple-element.433, f32[1024,256]{1,0:T(8,128)} %get-tuple-element.434, f32[3,3]{1,0:T(4,128)S(1)} %fusion.90, f32[8,3,1024]{2,0,1:T(8,128)S(1)} %get-tuple-element.472, pred[]{:T(512)S(6)} %compare.15, ...), kind=kOutput, calls=%fused_computation.37.clone.1 | convolution fusion | flops 233619456 | bytes 7563269 | tf_op jit(solution)/shard_map/while/body/eval_jaxpr/abts,kbs->kat/dot_general | solution.py:61
  763.4 10.5 %fusion.91 = f32[8,3,1024]{2,0,1:T(8,128)S(1)} fusion(f32[3,1024,256]{2,1,0:T(8,128)} %get-tuple-element.432, f32[3,1024,256]{2,1,0:T(8,128)S(1)} %get-tuple-element.433, f32[1024,256]{1,0:T(8,128)} %get-tuple-element.434, f32[3,3]{1,0:T(4,128)S(1)} %fusion.90, f32[8,3,1024]{2,0,1:T(8,128)S(1)} %get-tuple-element.472, pred[]{:T(512)S(6)} %compare.15, ...), kind=kOutput, calls=%fused_computation.37.clone.1 | convolution fusion | flops 233619456 | bytes 7563269 | tf_op jit(solution)/shard_map/while/body/eval_jaxpr/abts,kbs->kat/dot_general | solution.py:61
  778.5 10.5 %fusion.91 = f32[8,3,1024]{2,0,1:T(8,128)S(1)} fusion(f32[3,1024,256]{2,1,0:T(8,128)} %get-tuple-element.432, f32[3,1024,256]{2,1,0:T(8,128)S(1)} %get-tuple-element.433, f32[1024,256]{1,0:T(8,128)} %get-tuple-element.434, f32[3,3]{1,0:T(4,128)S(1)} %fusion.90, f32[8,3,1024]{2,0,1:T(8,128)S(1)} %get-tuple-element.472, pred[]{:T(512)S(6)} %compare.15, ...), kind=kOutput, calls=%fused_computation.37.clone.1 | convolution fusion | flops 233619456 | bytes 7563269 | tf_op jit(solution)/shard_map/while/body/eval_jaxpr/abts,kbs->kat/dot_general | solution.py:61
  793.6 10.5 %fusion.91 = f32[8,3,1024]{2,0,1:T(8,128)S(1)} fusion(f32[3,1024,256]{2,1,0:T(8,128)} %get-tuple-element.432, f32[3,1024,256]{2,1,0:T(8,128)S(1)} %get-tuple-element.433, f32[1024,256]{1,0:T(8,128)} %get-tuple-element.434, f32[3,3]{1,0:T(4,128)S(1)} %fusion.90, f32[8,3,1024]{2,0,1:T(8,128)S(1)} %get-tuple-element.472, pred[]{:T(512)S(6)} %compare.15, ...), kind=kOutput, calls=%fused_computation.37.clone.1 | convolution fusion | flops 233619456 | bytes 7563269 | tf_op jit(solution)/shard_map/while/body/eval_jaxpr/abts,kbs->kat/dot_general | solution.py:61
  804.8 105.6 %all-reduce.5.cloned.1.call-done = f32[8,3,1024]{2,0,1:T(8,128)} async-done(((f32[8,3,1024]{2,0,1:T(8,128)}), f32[8,3,1024]{2,0,1:T(8,128)}) %all-reduce.5.cloned.1.call-update) | async-done | bytes 98320 | tf_op jit(solution)/shard_map/psum | solution.py:66
  912.2 104.0 %psum.55 = f32[8,8]{0,1:T(8,128)S(1)} all-reduce(f32[8,8]{0,1:T(8,128)S(1)} %convolution_bitcast_fusion), channel_id=1, replica_groups=mesh['row'=16,'col'=32] {'row','col'}, use_global_device_ids=true, to_apply=%region_14.17 | all-reduce | flops 64 | bytes 512 | tf_op jit(solution)/shard_map/psum | solution.py:79
  (131 shorter events, 85.2 us)
Async XLA Ops:
  7.2 56.4 %copy-start = (f32[8,3,64]{2,0,1:T(8,128)S(1)}, f32[8,3,64]{2,0,1:T(8,128)}, u32[]{:S(2)}) copy-start(f32[8,3,64]{2,0,1:T(8,128)} %param.10) | copy-start | bytes 18436
  7.2 419.9 %all-reduce.3.cloned.1.call-start = ((), (), s32[]{:S(2)}) async-start(), calls=%async_computation | async-start | bytes 196608 | tf_op jit(solution)/shard_map/psum | solution.py:66
  323.9 0.6 copy-start.3
  324.6 585.8 %all-reduce.5.cloned.1.call-start = ((), (), s32[]{:S(2)}) async-start(), calls=%async_computation.1 | async-start | bytes 196608 | tf_op jit(solution)/shard_map/psum | solution.py:66
  636.4 379.7 %copy-start.1 = (f32[8,3,64]{2,0,1:T(8,128)}, f32[8,3,64]{2,0,1:T(8,128)S(1)}, u32[]{:S(2)}) copy-start(f32[8,3,64]{2,0,1:T(8,128)S(1)} %fusion.61) | copy-start | bytes 18436
  804.1 0.6 copy-start.2
Sparse Core Ops, SparseCore 0:
  324.7 102.2 all-reduce.2
  804.9 105.5 all-reduce.4
